TPU v7x, 32 devices: a whole 2x2x4 slice. The times are simulated.
32 devices in a mesh: groups: 2 (over y), seq: 4 (over z), head: 2 (over x), sub: 2 (over core).
Axes of the slice: x: 2, y: 2, z: 4, core: 2. Of those that a mesh axis runs over, the one named last changes fastest.
Arguments:
- tokens: bfloat16 [4096, 3072], P(('groups', 'seq')), parts along dimension 0, may hold values from -6 to 6
- modulation: float32 [3, 3072], replicated, may hold values from -4 to 4
- w_qkv: bfloat16 [3072, 8, 768], P('seq', ('head', 'sub')), may hold values from -0.15625 to 0.15625
- w_out: bfloat16 [2048, 3072], P('seq', ('head', 'sub')), may hold values from -0.125 to 0.125
- pattern: int32 [32, 4], P(('groups', 'seq')), parts along dimension 0, may hold values from 0 to 15, as said below
- counts: int32 [32], P(('groups', 'seq')), parts along dimension 0, may hold values from 1 to 4, as said below
- spatial_mask: int32 [8, 4, 4], P(('groups', 'seq')), parts along dimension 0, may hold values from 0 to 1, as said below
Outputs:
- update: bfloat16 [4096, 3072], P(('groups', 'seq'), ('head', 'sub')), parts along dimension 0
There are 2 independent parts, one for each index of `groups`. A program takes and returns all parts, laid end to end along the dimension named above; an argument that names none is the same for every part. Nothing has to cross between parts.
Inputs may be any that keep to these rules, and one draw needn't show every extreme that they name: pattern[b, 0] = b; each further entry of row b is b plus a nonzero offset of size at most 2, the offsets of one row different, clipped to the blocks of the video. `counts`: blocks with a count above one all lie in one cyclic run of half of the 16 blocks. `spatial_mask`: every diagonal entry is 1.
All inputs are finite; a program needn't handle non-finite values.
Results may differ from a plain program's by a relative error of at most 0.012.
The roundings to bfloat16 on the way count: a program that leaves them out, or rounds other values in their place, can miss the bound.
Values may be sent and summed in bfloat16 or wider, within the bound.
A program may use at most 128 MiB of HBM per device.

v0:
```python
import math
import jax
import jax.numpy as jnp
from jax import lax
from jax.sharding import PartitionSpec as P

BLOCK = 128
WIN = 2
EPSILON = 1e-06


def with_halo(cells, sides, width):
    for axis, dim in sides:
        count = lax.axis_size(axis)
        ends = count - 1
        head = lax.slice_in_dim(cells, 0, width, axis=dim)
        tail = lax.slice_in_dim(cells, cells.shape[dim] - width, cells.shape[dim], axis=dim)
        cells = jnp.concatenate(
            [
                lax.ppermute(tail, axis, [(i, (i + 1) % count) for i in range(ends)]),
                cells,
                lax.ppermute(head, axis, [((i + 1) % count, i) for i in range(ends)]),
            ],
            axis=dim,
        )
    return cells


def modulate(tokens, modulation):
    values = tokens.astype(jnp.float32)
    center = jnp.mean(values, axis=-1, keepdims=True)
    spread = jnp.mean(jnp.square(values - center), axis=-1, keepdims=True)
    normed = (values - center) * lax.rsqrt(spread + EPSILON)
    return (normed * (1.0 + modulation[1]) + modulation[0]).astype(jnp.bfloat16)


def shards(tokens, modulation, w_qkv, w_out, pattern, counts, spatial_mask):
    row_count, feature_width = tokens.shape
    pairs_local = w_qkv.shape[1]
    head_size = w_qkv.shape[2] // 6
    frames_local = spatial_mask.shape[0]
    positions = row_count // frames_local
    slot_total = pattern.shape[1]
    scale_factor = 1.0 / math.sqrt(head_size)
    hidden = modulate(tokens, modulation)
    piece = lax.all_gather(w_qkv, "seq", axis=0, tiled=True)
    projected = jnp.dot(
        hidden, piece.reshape(piece.shape[0], -1), preferred_element_type=jnp.float32
    )
    whole_out = lax.all_gather(w_out, "seq", axis=0, tiled=True)
    packed = projected.astype(jnp.bfloat16).reshape(
        frames_local, positions, pairs_local, 6 * head_size
    )
    temporal_in = packed[..., : 3 * head_size].transpose(1, 0, 2, 3)
    received = lax.all_to_all(temporal_in, "seq", split_axis=0, concat_axis=1, tiled=True)
    position_span, frame_total, items, _ = received.shape
    relaid = received.reshape(position_span * frame_total, items, 3 * head_size)
    extended = with_halo(relaid[:, :, head_size:], (("seq", 0),), WIN * BLOCK)
    block_count = position_span * frame_total // BLOCK
    key_table = extended.reshape(block_count + 2 * WIN, BLOCK, items, 2 * head_size)
    queries = relaid[:, :, :head_size].reshape(block_count, BLOCK, items, head_size)
    offsets = pattern - (lax.axis_index("seq") * block_count - WIN)

    def slot_step(slot_index, state_pair):
        numerator, denominator = state_pair
        chosen = lax.dynamic_index_in_dim(offsets, slot_index, 1, keepdims=False)
        picked = jnp.take(key_table, chosen, axis=0)
        scores = (
            jnp.einsum(
                "bqnc,bknc->bnqk",
                queries,
                picked[..., :head_size],
                preferred_element_type=jnp.float32,
            )
            * scale_factor
        )
        alive = (slot_index < counts).astype(jnp.float32)
        weights = jnp.exp(scores) * alive[:, None, None, None]
        numerator = numerator + jnp.einsum(
            "bnqk,bknc->bnqc",
            weights.astype(jnp.bfloat16),
            picked[..., head_size:],
            preferred_element_type=jnp.float32,
        )
        return (numerator, denominator + jnp.sum(weights, axis=-1))

    start_state = (
        jnp.zeros((block_count, items, BLOCK, head_size), jnp.float32),
        jnp.zeros((block_count, items, BLOCK), jnp.float32),
    )
    numerator, denominator = lax.fori_loop(0, slot_total, slot_step, start_state)
    outcome = (numerator / denominator[..., None]).astype(jnp.bfloat16)
    outcome = outcome.transpose(0, 2, 1, 3).reshape(position_span, frame_total, items, head_size)
    temporal_out = lax.all_to_all(outcome, "seq", split_axis=1, concat_axis=0, tiled=True)
    spatial = packed[..., 3 * head_size :]
    blocks_frame = positions // BLOCK
    scores = (
        jnp.einsum(
            "fpnc,fqnc->fnpq",
            spatial[..., :head_size],
            spatial[..., head_size : 2 * head_size],
            preferred_element_type=jnp.float32,
        )
        * scale_factor
    )
    keep = spatial_mask.astype(jnp.float32)[:, None, :, None, :, None]
    weights = (
        jnp.exp(scores).reshape(frames_local, pairs_local, blocks_frame, BLOCK, blocks_frame, BLOCK)
        * keep
    )
    weights = weights.reshape(frames_local, pairs_local, positions, positions)
    denominator = jnp.sum(weights, axis=-1)
    numerator = jnp.einsum(
        "fnpq,fqnc->fpnc",
        weights.astype(jnp.bfloat16),
        spatial[..., 2 * head_size :],
        preferred_element_type=jnp.float32,
    )
    spatial_out = (numerator / denominator.transpose(0, 2, 1)[..., None]).astype(jnp.bfloat16)
    attention = jnp.concatenate([temporal_out.transpose(1, 0, 2, 3), spatial_out], axis=-1)
    attention = attention.reshape(row_count, pairs_local, 2 * head_size)
    out_width = whole_out.shape[1]
    mixed = jnp.dot(
        lax.all_gather(attention, ("head", "sub"), axis=1, tiled=True).reshape(row_count, -1),
        whole_out,
        preferred_element_type=jnp.float32,
    )
    gate_slice = lax.dynamic_slice_in_dim(
        modulation[2], lax.axis_index(("head", "sub")) * out_width, out_width, 0
    )
    return (gate_slice * mixed).astype(jnp.bfloat16)


def solution(mesh):
    return jax.shard_map(
        shards,
        mesh=mesh,
        in_specs=(
            P(("groups", "seq"), None),
            P(),
            P("seq", ("head", "sub"), None),
            P("seq", ("head", "sub")),
            P(("groups", "seq"), None),
            P(("groups", "seq")),
            P(("groups", "seq"), None, None),
        ),
        out_specs=P(("groups", "seq"), ("head", "sub")),
        check_vma=False,
    )
```

profile of v0, /device:TPU:0, one launch (start us, length us, event | category | flops | bytes accessed | tf_op | source)
XLA Modules:
  0.0 360.5 jit_solution(18314034296797499365)
XLA Ops:
  6.5 0.7 all-gather.5.cloned.1.call-update
  7.3 2.6 convert_reduce_fusion
  9.9 1.0 fusion.8
  10.9 167.5 %all-gather.5.cloned.1.call-done = bf16[3072,2,768]{2,1,0:T(2,128)(2,1)} async-done(((bf16[768,2,768]{2,1,0:T(2,128)(2,1)}), bf16[3072,2,768]{2,1,0:T(2,128)(2,1)}) %all-gather.5.cloned.1.call-update) | async-done | bytes 9437200 | tf_op jit(solution)/shard_map/all_gather | solution.py:46
  178.4 9.0 %copy.65 = bf16[384,8,2,768]{3,1,2,0:T(8,128)(2,1)} copy(bf16[384,8,2,768]{3,2,1,0:T(2,128)(2,1)} %bitcast.76) | data formatting | bytes 18874368
  187.4 10.0 %fusion.18 = bf16[512,1536]{1,0:T(8,128)(2,1)} fusion(bf16[3072,1536]{1,0:T(8,128)(2,1)} %bitcast.77, bf16[512,3072]{1,0:T(8,128)(2,1)S(1)} %copy-done, f32[3072]{0:T(1024)S(1)} %bitcast.89, f32[3072]{0:T(1024)S(1)} %bitcast.90, f32[512]{0:T(512)S(1)} %add_rsqrt_fusion, f32[512]{0:T(512)S(1)} %broadcast_multiply_fusion), kind=kOutput, calls=%fused_computation.28 | convolution fusion | flops 4842061824 | bytes 14184448 | tf_op jit(solution)/shard_map/dot_general | solution.py:47
  197.4 3.6 %reshape.85 = bf16[1,512,2,768]{3,2,1,0:T(2,128)(2,1)S(1)} reshape(bf16[512,1536]{1,0:T(8,128)(2,1)} %fusion.18) | data formatting | bytes 3145728 | tf_op jit(solution)/shard_map/reshape | solution.py:51
  201.1 1.4 slice_bitcast_fusion
  202.5 3.5 all-to-all-start
  206.1 20.4 %all-to-all-done = bf16[512,1,2,384]{3,2,1,0:T(2,128)(2,1)S(1)} async-done(((bf16[512,1,2,384]{3,2,1,0:T(2,128)(2,1)}), bf16[512,1,2,384]{3,2,1,0:T(2,128)(2,1)S(1)}, u32[]{:S(2)}, u32[]{:S(2)}) %all-to-all-start) | async-done | bytes 786464 | tf_op jit(solution)/shard_map/all_to_all | solution.py:55
  226.5 1.5 copy.81
  228.0 1.6 reshape.86
  229.6 0.9 fusion.34
  230.5 2.0 collective-permute-start
  232.5 1.3 collective-permute-start.1
  233.9 0.2 mul.111
  234.1 1.1 copy.80
  235.1 1.2 fusion.33
  236.5 0.7 collective-permute-done
  237.2 4.8 %collective-permute-done.1 = bf16[256,2,256]{2,0,1:T(8,128)(2,1)} collective-permute-done((bf16[256,2,256]{2,0,1:T(8,128)(2,1)}, bf16[256,2,256]{2,0,1:T(8,128)(2,1)}, u32[]{:S(2)}, u32[]{:S(2)}) %collective-permute-start.1) | collective-permute-done | bytes 262176 | tf_op jit(solution)/shard_map/ppermute | solution.py:22
  242.0 1.1 pad_maximum_fusion
  243.2 5.9 %while.16 = (s32[]{:T(128)}, f32[4,2,128,128]{3,2,1,0:T(8,128)S(1)}, f32[4,2,128]{2,1,0:T(2,128)S(1)}, s32[4,4]{0,1:T(4,128)S(1)}, bf16[8,128,2,256]{3,1,2,0:T(8...) while((s32[]{:T(128)}, ...), condition=%wide.region_4.5_spmd.clone, body=%wide.region_2.4_spmd.clone.sunk | while | flops 68159520 | bytes 4477664 | solution.py:91
  243.3 0.6 gather_fusion
  244.0 0.3 fusion.48
  244.4 0.3 convolution_add_fusion.2
  244.8 0.6 gather_fusion
  245.5 0.3 fusion.48
  245.8 0.3 convolution_add_fusion.2
  246.3 0.6 gather_fusion
  247.0 0.3 fusion.48
  247.3 0.3 convolution_add_fusion.2
  247.8 0.6 gather_fusion
  248.5 0.3 fusion.48
  248.8 0.3 convolution_add_fusion.2
  249.2 0.2 fusion.28
  249.4 0.8 copy.51
  250.2 3.4 all-to-all-start.1
  253.6 0.2 all-gather.9.cloned.1.call-start
  253.8 1.9 fusion.21
  255.9 2.1 fusion.24
  258.0 3.4 all-to-all-done.1
  261.4 0.2 copy.52
  261.7 1.0 copy.58
  262.8 0.7 all-gather.7.cloned.1.call-update
  263.5 20.8 %all-gather.9.cloned.1.call-done = bf16[1,512,8,256]{3,1,0,2:T(8,128)(2,1)} async-done(((bf16[1,512,2,256]{3,1,0,2:T(8,128)(2,1)}), bf16[1,512,8,256]{3,1,0,2:T(8,128)(2,1)}) %all-gather.9.cloned.1.call-update) | async-done | bytes 2097168 | tf_op jit(solution)/shard_map/all_gather | solution.py:124
  284.3 2.9 copy.59
  287.2 62.2 %all-gather.7.cloned.1.call-done = bf16[2048,768]{1,0:T(8,128)(2,1)} async-done(((bf16[512,768]{1,0:T(8,128)(2,1)}), bf16[2048,768]{1,0:T(8,128)(2,1)}) %all-gather.7.cloned.1.call-update) | async-done | bytes 3145744 | tf_op jit(solution)/shard_map/all_gather | solution.py:50
  349.3 4.6 %multiply_convert_fusion = bf16[512,768]{1,0:T(8,128)(2,1)} fusion(bf16[512,2048]{0,1:T(8,128)(2,1)S(1)} %bitcast.84, bf16[2048,768]{1,0:T(8,128)(2,1)} %all-gather.7.cloned.1.call-done, f32[768]{0:T(1024)S(1)} %dynamic-slice_reduce_fusion), kind=kOutput, calls=%fused_computation.32 | convolution fusion | flops 1611399168 | bytes 6032384 | tf_op jit(solution)/shard_map/dot_general | solution.py:123
  (55 shorter events, 1.4 us)
Async XLA Ops:
  6.5 171.9 %all-gather.5.cloned.1.call-start = ((), (), s32[]{:S(2)}) async-start(), calls=%async_computation.2 | async-start | bytes 11796480 | tf_op jit(solution)/shard_map/all_gather | solution.py:46
  6.5 3.3 copy-start
  9.9 1.0 copy-start.3
  201.0 5.0 %copy-start.4 = (s32[4,4]{1,0:T(4,128)S(1)}, s32[4,4]{1,0:T(4,128)}, u32[]{:S(2)}) copy-start(s32[4,4]{1,0:T(4,128)} %param.13) | copy-start | bytes 196
  201.1 5.0 %copy-start.5 = (s32[1,4,4]{2,1,0:T(4,128)S(1)}, s32[1,4,4]{2,1,0:T(4,128)}, u32[]{:S(2)}) copy-start(s32[1,4,4]{2,1,0:T(4,128)} %param.15) | copy-start | bytes 196
  202.5 24.0 %all-to-all-start = ((bf16[512,1,2,384]{3,2,1,0:T(2,128)(2,1)}), bf16[512,1,2,384]{3,2,1,0:T(2,128)(2,1)S(1)}, u32[]{:S(2)}, u32[]{:S(2)}) async-start(bf16[512,1,2,384]{3,2,1,0:T(2,128)(2,1)} %slice_bitcast_fusion), calls=%async_computation | async-start | bytes 1572864 | tf_op jit(solution)/shard_map/all_to_all | solution.py:55
  230.5 6.8 %collective-permute-start = (bf16[256,2,256]{2,0,1:T(8,128)(2,1)}, bf16[256,2,256]{2,0,1:T(8,128)(2,1)}, u32[]{:S(2)}, u32[]{:S(2)}) collective-permute-start(bf16[256,2,256]{2,0,1:T(8,128)(2,1)} %get-tuple-element.198), channel_id=1, source_target_pairs={{0,4},{4,8},{8,12},{1,5},{5,9},{9,13},{2,6},{6,10},{10,14},{3,7},{... | collective-permute-start | bytes 786440 | tf_op jit(solution)/shard_map/ppermute | solution.py:20
  232.5 9.6 %collective-permute-start.1 = (bf16[256,2,256]{2,0,1:T(8,128)(2,1)}, bf16[256,2,256]{2,0,1:T(8,128)(2,1)}, u32[]{:S(2)}, u32[]{:S(2)}) collective-permute-start(bf16[256,2,256]{2,0,1:T(8,128)(2,1)} %get-tuple-element.199), channel_id=1, source_target_pairs={{4,0},{8,4},{12,8},{5,1},{9,5},{13,9},{6,2},{10,6},{14,10},{7,3},{... | collective-permute-start | bytes 786440 | tf_op jit(solution)/shard_map/ppermute | solution.py:22
  236.4 6.8 %copy-start.6 = (s32[4]{0:T(128)S(1)}, s32[4]{0:T(128)}, u32[]{:S(2)}) copy-start(s32[4]{0:T(128)} %param.14) | copy-start | bytes 52
  249.2 4.6 %copy-start.1 = (f32[64,8,4,128]{3,1,2,0:T(8,128)S(1)}, f32[64,8,4,128]{3,1,2,0:T(8,128)}, u32[]{:S(2)}) copy-start(f32[64,8,4,128]{3,1,2,0:T(8,128)} %copy.80) | copy-start | bytes 3145732
  249.4 6.3 %copy-start.2 = (bf16[1,512,2,128]{3,2,1,0:T(2,128)(2,1)S(1)}, bf16[1,512,2,128]{3,2,1,0:T(2,128)(2,1)}, u32[]{:S(2)}) copy-start(bf16[1,512,2,128]{3,2,1,0:T(2,128)(2,1)} %get-tuple-element.195) | copy-start | bytes 786436
  250.2 11.2 %all-to-all-start.1 = ((bf16[128,4,2,128]{3,0,2,1:T(8,128)(2,1)}), bf16[128,4,2,128]{3,0,2,1:T(8,128)(2,1)S(1)}, u32[]{:S(2)}, u32[]{:S(2)}) async-start(bf16[128,4,2,128]{3,0,2,1:T(8,128)(2,1)} %copy.51), calls=%async_computation.1 | async-start | bytes 524288 | tf_op jit(solution)/shard_map/all_to_all | solution.py:94
  253.6 30.7 %all-gather.9.cloned.1.call-start = ((), (), s32[]{:S(2)}) async-start(), calls=%async_computation.4 | async-start | bytes 2621440 | tf_op jit(solution)/shard_map/all_gather | solution.py:124
  262.8 86.6 %all-gather.7.cloned.1.call-start = ((), (), s32[]{:S(2)}) async-start(), calls=%async_computation.3 | async-start | bytes 3932160 | tf_op jit(solution)/shard_map/all_gather | solution.py:50
Sparse Core Ops, SparseCore 0:
  8.9 169.4 all-gather.4
  262.9 21.3 all-gather.8
  285.9 63.4 all-gather.6
where the time goes:
time: 361 us; the launch traced here: 360 us
  waiting for transfers between devices  281 us (78%)
  local copies, waits for them, and re-layouts  28.3 us (8%)
  matrix products  21.3 us (6%)
  between operations  13.4 us (4%)
  starting transfers between devices  10.5 us (3%)
  other arithmetic  5.58 us (2%)
    all_gather x1, waiting for transfers between devices, shards(): piece = lax.all_gather(w_qkv, 'seq', axis=0, tiled=True)  168 us
    all_gather x1, waiting for transfers between devices, shards(): whole_out = lax.all_gather(w_out, 'seq', axis=0, tiled=True)  62.2 us
    all_gather x1, waiting for transfers between devices, shards(): lax.all_gather(attention, ('head', 'sub'), axis=1, tiled=True)  20.8 us
    all_to_all x1, waiting for transfers between devices, shards(): lax.all_to_all(temporal_in, 'seq', split_axis=0, concat_axis=1, tiled=True)  20.4 us
    unnamed x20, local copies, waits for them, and re-layouts  10.5 us
    dot_general x1, matrix products, shards(): jnp.dot(hidden, piece.reshape(piece.shape[0], -1), preferred_element_type...  10 us
  transfers between devices with their start and end apart: 7, of which 7 were waited for; matrix products, arithmetic and copies ran while one was open for 4% of the time, Pallas kernels for 0%

commit v1 on v0

--- a/solution.py
+++ b/solution.py
@@ -7,6 +7,12 @@
 BLOCK = 128
 WIN = 2
 EPSILON = 1e-06
+
+
+def gathered_along(x, axis, dim):
+    parts = lax.all_gather(x, axis, axis=0, tiled=False)
+    out = jnp.concatenate(parts, axis=dim)
+    return out
 
 
 def with_halo(cells, sides, width):
@@ -121,7 +127,7 @@
     attention = attention.reshape(row_count, pairs_local, 2 * head_size)
     out_width = whole_out.shape[1]
     mixed = jnp.dot(
-        lax.all_gather(attention, ("head", "sub"), axis=1, tiled=True).reshape(row_count, -1),
+        gathered_along(attention, ("head", "sub"), 1).reshape(row_count, -1),
         whole_out,
         preferred_element_type=jnp.float32,
     )

time: 361 us -> 361 us (level)
  no operation moved by 1% of the time
where the time goes in v1:
time: 361 us; the launch traced here: 360 us
  waiting for transfers between devices  281 us (78%)
  local copies, waits for them, and re-layouts  28.2 us (8%)
  matrix products  21.3 us (6%)
  between operations  13.4 us (4%)
  starting transfers between devices  10.5 us (3%)
  other arithmetic  5.58 us (2%)
    all_gather x1, waiting for transfers between devices, shards(): piece = lax.all_gather(w_qkv, 'seq', axis=0, tiled=True)  168 us
    all_gather x1, waiting for transfers between devices, shards(): whole_out = lax.all_gather(w_out, 'seq', axis=0, tiled=True)  62.3 us
    all_gather x1, waiting for transfers between devices, gathered_along(): parts = lax.all_gather(x, axis, axis=0, tiled=False)  20.8 us
    all_to_all x1, waiting for transfers between devices, shards(): lax.all_to_all(temporal_in, 'seq', split_axis=0, concat_axis=1, tiled=True)  20.4 us
    unnamed x20, local copies, waits for them, and re-layouts  10.5 us
    dot_general x1, matrix products, shards(): jnp.dot(hidden, piece.reshape(piece.shape[0], -1), preferred_element_type...  10 us
  transfers between devices with their start and end apart: 7, of which 7 were waited for; matrix products, arithmetic and copies ran while one was open for 4% of the time, Pallas kernels for 0%

profile of v1, /device:TPU:0, one launch (start us, length us, event | category | flops | bytes accessed | tf_op | source)
XLA Modules:
  0.0 360.5 jit_solution(11769321107834531793)
XLA Ops:
  6.5 0.7 all-gather.4.cloned.1.call-update
  7.3 2.6 convert_reduce_fusion
  9.9 1.0 fusion.8
  10.9 167.5 %all-gather.4.cloned.1.call-done = bf16[3072,2,768]{2,1,0:T(2,128)(2,1)} async-done(((bf16[768,2,768]{2,1,0:T(2,128)(2,1)}), bf16[3072,2,768]{2,1,0:T(2,128)(2,1)}) %all-gather.4.cloned.1.call-update) | async-done | bytes 9437200 | tf_op jit(solution)/shard_map/all_gather | solution.py:52
  178.4 9.0 %copy.65 = bf16[384,8,2,768]{3,1,2,0:T(8,128)(2,1)} copy(bf16[384,8,2,768]{3,2,1,0:T(2,128)(2,1)} %bitcast.78) | data formatting | bytes 18874368
  187.4 10.0 %fusion.18 = bf16[512,1536]{1,0:T(8,128)(2,1)} fusion(bf16[3072,1536]{1,0:T(8,128)(2,1)} %bitcast.79, bf16[512,3072]{1,0:T(8,128)(2,1)S(1)} %copy-done, f32[3072]{0:T(1024)S(1)} %bitcast.91, f32[3072]{0:T(1024)S(1)} %bitcast.92, f32[512]{0:T(512)S(1)} %add_rsqrt_fusion, f32[512]{0:T(512)S(1)} %broadcast_multiply_fusion), kind=kOutput, calls=%fused_computation.28 | convolution fusion | flops 4842061824 | bytes 14184448 | tf_op jit(solution)/shard_map/dot_general | solution.py:53
  197.4 3.6 %reshape.82 = bf16[1,512,2,768]{3,2,1,0:T(2,128)(2,1)S(1)} reshape(bf16[512,1536]{1,0:T(8,128)(2,1)} %fusion.18) | data formatting | bytes 3145728 | tf_op jit(solution)/shard_map/reshape | solution.py:57
  201.1 1.4 slice_bitcast_fusion
  202.5 3.5 all-to-all-start
  206.1 20.4 %all-to-all-done = bf16[512,1,2,384]{3,2,1,0:T(2,128)(2,1)S(1)} async-done(((bf16[512,1,2,384]{3,2,1,0:T(2,128)(2,1)}), bf16[512,1,2,384]{3,2,1,0:T(2,128)(2,1)S(1)}, u32[]{:S(2)}, u32[]{:S(2)}) %all-to-all-start) | async-done | bytes 786464 | tf_op jit(solution)/shard_map/all_to_all | solution.py:61
  226.5 1.5 copy.81
  228.0 1.6 reshape.83
  229.6 0.9 fusion.34
  230.5 2.0 collective-permute-start
  232.5 1.3 collective-permute-start.1
  233.9 0.2 mul.111
  234.1 1.1 copy.80
  235.1 1.2 fusion.33
  236.5 0.7 collective-permute-done
  237.2 4.8 %collective-permute-done.1 = bf16[256,2,256]{2,0,1:T(8,128)(2,1)} collective-permute-done((bf16[256,2,256]{2,0,1:T(8,128)(2,1)}, bf16[256,2,256]{2,0,1:T(8,128)(2,1)}, u32[]{:S(2)}, u32[]{:S(2)}) %collective-permute-start.1) | collective-permute-done | bytes 262176 | tf_op jit(solution)/shard_map/ppermute | solution.py:28
  242.0 1.1 pad_maximum_fusion
  243.2 5.9 %while.16 = (s32[]{:T(128)}, f32[4,2,128,128]{3,2,1,0:T(8,128)S(1)}, f32[4,2,128]{2,1,0:T(2,128)S(1)}, s32[4,4]{0,1:T(4,128)S(1)}, bf16[8,128,2,256]{3,1,2,0:T(8...) while((s32[]{:T(128)}, ...), condition=%wide.region_4.5_spmd.clone, body=%wide.region_2.4_spmd.clone.sunk | while | flops 68159520 | bytes 4477664 | solution.py:97
  243.3 0.6 gather_fusion
  244.0 0.3 fusion.48
  244.4 0.3 convolution_add_fusion.2
  244.8 0.6 gather_fusion
  245.5 0.3 fusion.48
  245.8 0.3 convolution_add_fusion.2
  246.3 0.6 gather_fusion
  247.0 0.3 fusion.48
  247.3 0.3 convolution_add_fusion.2
  247.8 0.6 gather_fusion
  248.5 0.3 fusion.48
  248.8 0.3 convolution_add_fusion.2
  249.2 0.2 fusion.28
  249.4 0.8 copy.51
  250.2 3.4 all-to-all-start.1
  253.6 0.2 all-gather.6.cloned.1.call-start
  253.8 1.9 fusion.21
  255.9 2.1 fusion.24
  258.0 3.4 all-to-all-done.1
  261.4 0.2 copy.52
  261.7 1.0 copy.58
  262.8 0.7 all-gather.8.cloned.1.call-update
  263.5 20.8 %all-gather.6.cloned.1.call-done = bf16[4,512,2,256]{3,1,2,0:T(8,128)(2,1)} async-done(((bf16[1,512,2,256]{3,1,2,0:T(8,128)(2,1)}), bf16[4,512,2,256]{3,1,2,0:T(8,128)(2,1)}) %all-gather.6.cloned.1.call-update) | async-done | bytes 2097168 | tf_op jit(solution)/shard_map/all_gather | solution.py:13
  284.3 2.8 copy.59
  287.1 62.3 %all-gather.8.cloned.1.call-done = bf16[2048,768]{1,0:T(8,128)(2,1)} async-done(((bf16[512,768]{1,0:T(8,128)(2,1)}), bf16[2048,768]{1,0:T(8,128)(2,1)}) %all-gather.8.cloned.1.call-update) | async-done | bytes 3145744 | tf_op jit(solution)/shard_map/all_gather | solution.py:56
  349.3 4.6 %multiply_convert_fusion = bf16[512,768]{1,0:T(8,128)(2,1)} fusion(bf16[512,2048]{0,1:T(8,128)(2,1)S(1)} %bitcast.86, bf16[2048,768]{1,0:T(8,128)(2,1)} %all-gather.8.cloned.1.call-done, f32[768]{0:T(1024)S(1)} %dynamic-slice_reduce_fusion), kind=kOutput, calls=%fused_computation.32 | convolution fusion | flops 1611399168 | bytes 6032384 | tf_op jit(solution)/shard_map/dot_general | solution.py:129
  (55 shorter events, 1.4 us)
Async XLA Ops:
  6.5 171.9 %all-gather.4.cloned.1.call-start = ((), (), s32[]{:S(2)}) async-start(), calls=%async_computation.2 | async-start | bytes 11796480 | tf_op jit(solution)/shard_map/all_gather | solution.py:52
  6.5 3.3 copy-start
  9.9 1.0 copy-start.3
  201.0 5.0 %copy-start.4 = (s32[4,4]{1,0:T(4,128)S(1)}, s32[4,4]{1,0:T(4,128)}, u32[]{:S(2)}) copy-start(s32[4,4]{1,0:T(4,128)} %param.13) | copy-start | bytes 196
  201.1 5.0 %copy-start.5 = (s32[1,4,4]{2,1,0:T(4,128)S(1)}, s32[1,4,4]{2,1,0:T(4,128)}, u32[]{:S(2)}) copy-start(s32[1,4,4]{2,1,0:T(4,128)} %param.15) | copy-start | bytes 196
  202.5 24.0 %all-to-all-start = ((bf16[512,1,2,384]{3,2,1,0:T(2,128)(2,1)}), bf16[512,1,2,384]{3,2,1,0:T(2,128)(2,1)S(1)}, u32[]{:S(2)}, u32[]{:S(2)}) async-start(bf16[512,1,2,384]{3,2,1,0:T(2,128)(2,1)} %slice_bitcast_fusion), calls=%async_computation | async-start | bytes 1572864 | tf_op jit(solution)/shard_map/all_to_all | solution.py:61
  230.5 6.8 %collective-permute-start = (bf16[256,2,256]{2,0,1:T(8,128)(2,1)}, bf16[256,2,256]{2,0,1:T(8,128)(2,1)}, u32[]{:S(2)}, u32[]{:S(2)}) collective-permute-start(bf16[256,2,256]{2,0,1:T(8,128)(2,1)} %get-tuple-element.198), channel_id=1, source_target_pairs={{0,4},{4,8},{8,12},{1,5},{5,9},{9,13},{2,6},{6,10},{10,14},{3,7},{... | collective-permute-start | bytes 786440 | tf_op jit(solution)/shard_map/ppermute | solution.py:26
  232.5 9.6 %collective-permute-start.1 = (bf16[256,2,256]{2,0,1:T(8,128)(2,1)}, bf16[256,2,256]{2,0,1:T(8,128)(2,1)}, u32[]{:S(2)}, u32[]{:S(2)}) collective-permute-start(bf16[256,2,256]{2,0,1:T(8,128)(2,1)} %get-tuple-element.199), channel_id=1, source_target_pairs={{4,0},{8,4},{12,8},{5,1},{9,5},{13,9},{6,2},{10,6},{14,10},{7,3},{... | collective-permute-start | bytes 786440 | tf_op jit(solution)/shard_map/ppermute | solution.py:28
  236.4 6.8 %copy-start.6 = (s32[4]{0:T(128)S(1)}, s32[4]{0:T(128)}, u32[]{:S(2)}) copy-start(s32[4]{0:T(128)} %param.14) | copy-start | bytes 52
  249.2 4.6 %copy-start.1 = (f32[64,8,4,128]{3,1,2,0:T(8,128)S(1)}, f32[64,8,4,128]{3,1,2,0:T(8,128)}, u32[]{:S(2)}) copy-start(f32[64,8,4,128]{3,1,2,0:T(8,128)} %copy.80) | copy-start | bytes 3145732
  249.4 6.3 %copy-start.2 = (bf16[1,512,2,128]{3,2,1,0:T(2,128)(2,1)S(1)}, bf16[1,512,2,128]{3,2,1,0:T(2,128)(2,1)}, u32[]{:S(2)}) copy-start(bf16[1,512,2,128]{3,2,1,0:T(2,128)(2,1)} %get-tuple-element.195) | copy-start | bytes 786436
  250.2 11.2 %all-to-all-start.1 = ((bf16[128,4,2,128]{3,0,2,1:T(8,128)(2,1)}), bf16[128,4,2,128]{3,0,2,1:T(8,128)(2,1)S(1)}, u32[]{:S(2)}, u32[]{:S(2)}) async-start(bf16[128,4,2,128]{3,0,2,1:T(8,128)(2,1)} %copy.51), calls=%async_computation.1 | async-start | bytes 524288 | tf_op jit(solution)/shard_map/all_to_all | solution.py:100
  253.6 30.7 %all-gather.6.cloned.1.call-start = ((), (), s32[]{:S(2)}) async-start(), calls=%async_computation.3 | async-start | bytes 2621440 | tf_op jit(solution)/shard_map/all_gather | solution.py:13
  262.8 86.6 %all-gather.8.cloned.1.call-start = ((), (), s32[]{:S(2)}) async-start(), calls=%async_computation.4 | async-start | bytes 3932160 | tf_op jit(solution)/shard_map/all_gather | solution.py:56
Sparse Core Ops, SparseCore 0:
  8.9 169.4 all-gather.3
  262.9 21.3 all-gather.5
  285.9 63.4 all-gather.7
